TPU v7x, 768 devices: a whole 4x8x12 slice. The times are simulated.
768 devices in a mesh: replica: 32 (over y, x), owner: 6 (over z_lo, core), tensor: 4 (over z_hi).
Axes of the slice: x: 4, y: 8, z: 12 (z_hi: 4, z_lo: 3; z = z_hi * 3 + z_lo), core: 2. Of those that a mesh axis runs over, the one named last changes fastest.
Arguments:
- grad_partial: bfloat16 [192, 24, 512, 512], P(('replica', 'owner'), 'tensor'), may hold values from -1 to 1
- owner_table: int32 [4, 6], P('tensor'), may hold values from 0 to 5, each once within a row
- left_factor: float32 [6, 4, 512, 512], P('owner', 'tensor'), may hold values from -1 to 4, as said below
- right_factor: float32 [6, 4, 512, 512], P('owner', 'tensor'), may hold values from -1 to 4, as said below
- left_precond: bfloat16 [6, 4, 512, 512], P('owner', 'tensor'), may hold values from -2 to 3, as said below
- right_precond: bfloat16 [6, 4, 512, 512], P('owner', 'tensor'), may hold values from -2 to 3, as said below
Outputs:
- direction: bfloat16 [24, 512, 512], P('tensor')
- new_left: float32 [6, 4, 512, 512], P('owner', 'tensor')
- new_right: float32 [6, 4, 512, 512], P('owner', 'tensor')
Inputs may be any that keep to these rules, and one draw needn't show every extreme that they name: `owner_table`: each row of the table is a permutation: every owner holds exactly one block of each tensor shard. `left_factor`: Symmetric. `right_factor`: Symmetric. `left_precond`: Symmetric. `right_precond`: Symmetric.
All inputs are finite; a program needn't handle non-finite values.
Results may differ from a plain program's by a relative error of at most 0.015.
Values may be sent and summed in bfloat16 or wider, within the bound.
No kernel may reach another device: no remote copies, remote signals or barrier semaphores. Data moves between devices by JAX's collectives and lax.ppermute only.
A program may use at most 32 MiB of HBM per device.

v0:
```python
import jax
import jax.numpy as jnp
from jax import lax
from jax.sharding import PartitionSpec as P

decay = 0.9
epsilon = 1e-06


def local(grad_partial, owner_table, left_factor, right_factor, left_precond, right_precond):
    table_row = owner_table[0]
    count = table_row.shape[0]
    positions = jnp.arange(count, dtype=jnp.int32)
    matches = table_row[None, :] == positions[:, None]
    inverse = jnp.sum(jnp.where(matches, positions[None, :], 0), axis=1)
    ordered = jnp.take(grad_partial[0], inverse, axis=0)
    mine = lax.psum_scatter(
        ordered.astype(jnp.float32).astype(jnp.bfloat16), "owner", scatter_dimension=0, tiled=True
    ).astype(jnp.float32)
    owned = lax.psum(mine[0], "replica").astype(jnp.bfloat16)
    half_product = jnp.dot(left_precond[0, 0], owned, preferred_element_type=jnp.float32).astype(
        jnp.bfloat16
    )
    full_product = jnp.dot(half_product, right_precond[0, 0], preferred_element_type=jnp.float32)
    scaled = (full_product * lax.rsqrt(jnp.mean(full_product * full_product) + epsilon)).astype(
        jnp.bfloat16
    )
    gathered = lax.all_gather(scaled[None], "owner", axis=0, tiled=True)
    direction = jnp.take(gathered, table_row, axis=0)
    outer_rows = lax.dot_general(
        owned, owned, (((1,), (1,)), ((), ())), preferred_element_type=jnp.float32
    )
    outer_cols = lax.dot_general(
        owned, owned, (((0,), (0,)), ((), ())), preferred_element_type=jnp.float32
    )
    new_left = (decay * left_factor[0, 0] + (1.0 - decay) * outer_rows)[None, None]
    new_right = (decay * right_factor[0, 0] + (1.0 - decay) * outer_cols)[None, None]
    return (direction, new_left, new_right)


def solution(mesh):
    placed = (
        P(("replica", "owner"), "tensor", None, None),
        P("tensor", None),
        P("owner", "tensor", None, None),
        P("owner", "tensor", None, None),
        P("owner", "tensor", None, None),
        P("owner", "tensor", None, None),
    )
    return jax.shard_map(
        local,
        mesh=mesh,
        in_specs=placed,
        out_specs=(
            P("tensor", None, None),
            P("owner", "tensor", None, None),
            P("owner", "tensor", None, None),
        ),
        check_vma=False,
    )
```

profile of v0, /device:TPU:1, one launch (start us, length us, event | category | flops | bytes accessed | tf_op | source)
XLA Modules:
  0.0 296.0 jit_solution(11297962628182446584)
XLA Ops:
  7.2 0.0 copy-start
  7.2 0.0 reduce-scatter.2.cloned.1.call-start
  7.2 0.9 select_reduce_fusion
  8.2 0.9 copy-done
  9.1 2.5 gather_fusion
  11.6 3.9 %broadcast_select_fusion.1 = bf16[6,512,512]{2,1,0:T(8,128)(2,1)} fusion(bf16[6,512,512]{2,1,0:T(8,128)(2,1)} %gather_fusion, pred[6]{0:T(512)(128)(4,1)S(1)} %compare_and_fusion.1), kind=kLoop, calls=%fused_computation.3 | loop fusion | flops 1572864 | bytes 6291462 | tf_op jit(solution)/shard_map/jit(_take)/select_n | solution.py:16
  15.5 0.0 reduce-scatter.2.cloned.1.call-update
  15.5 0.0 all-gather.3.cloned.1.call-start
  15.6 56.0 %reduce-scatter.2.cloned.1.call-done = bf16[1,512,512]{2,1,0:T(8,128)(2,1)} async-done(((bf16[6,512,512]{2,1,0:T(8,128)(2,1)}), bf16[1,512,512]{2,1,0:T(8,128)(2,1)}) %reduce-scatter.2.cloned.1.call-update) | async-done | bytes 524304 | tf_op jit(solution)/shard_map/reduce_scatter | solution.py:17
  71.6 2.1 bitcast_convert_fusion
  73.7 127.8 %all-reduce.1 = bf16[512,512]{1,0:T(8,128)(2,1)} all-reduce(f32[512,512]{1,0:T(8,128)} %bitcast_convert_fusion), channel_id=1, replica_groups=mesh['replica'=32,'owner'=6,'tensor'=4] {'replica'}, use_global_device_ids=true, to_apply=%region_2.4 | all-reduce | flops 262144 | bytes 1572864 | tf_op jit(solution)/shard_map/psum | solution.py:20
  201.6 3.8 %multiply_reduce_fusion = (f32[]{:T(128)}, f32[512,512]{1,0:T(8,128)}) fusion(bf16[1,1,512,512]{3,2,1,0:T(8,128)(2,1)} %param.13, bf16[1,1,512,512]{3,2,1,0:T(8,128)(2,1)} %param.12, bf16[512,512]{1,0:T(8,128)(2,1)} %all-reduce.1), kind=kOutput, calls=%fused_computation.13 | convolution fusion | flops 537657344 | bytes 2621444 | tf_op jit(solution)/shard_map/dot_general | solution.py:24
  206.1 2.1 multiply_convert_fusion
  208.2 0.0 all-gather.3.cloned.1.call-update
  208.3 0.0 copy-done.3
  208.3 0.0 copy-start.1
  208.3 0.0 copy-start.2
  208.3 3.1 %fusion.3 = f32[1,1,512,512]{3,2,1,0:T(8,128)} fusion(f32[1,1,512,512]{3,2,1,0:T(8,128)} %param.10, bf16[512,512]{1,0:T(8,128)(2,1)} %all-reduce.1), kind=kOutput, calls=%fused_computation.9 | convolution fusion | flops 269221888 | bytes 2621440 | tf_op jit(solution)/shard_map/dot_general | solution.py:30
  211.4 0.0 copy-done.1
  211.4 0.0 copy-done.2
  211.4 1.5 fusion.1
  212.9 67.9 %all-gather.3.cloned.1.call-done = bf16[3072,512]{1,0:T(8,128)(2,1)} async-done(((bf16[512,512]{1,0:T(8,128)(2,1)}), bf16[3072,512]{1,0:T(8,128)(2,1)}) %all-gather.3.cloned.1.call-update) | async-done | bytes 3145744 | tf_op jit(solution)/shard_map/all_gather | solution.py:28
  280.8 4.4 %gather_fusion.1 = bf16[6,512,512]{2,1,0:T(8,128)(2,1)} fusion(bf16[6,512,512]{2,1,0:T(8,128)(2,1)} %bitcast.34, s32[1024]{0:T(1024)S(1)} %pad_clamp_fusion), kind=kCustom, calls=%fused_computation.1.clone | custom fusion | bytes 6291480 | tf_op jit(solution)/shard_map/jit(_take)/gather | solution.py:29
  285.2 3.9 %broadcast_select_fusion = bf16[6,512,512]{2,1,0:T(8,128)(2,1)} fusion(bf16[6,512,512]{2,1,0:T(8,128)(2,1)} %gather_fusion.1, pred[6]{0:T(512)(128)(4,1)S(1)} %compare_and_fusion), kind=kLoop, calls=%fused_computation.2 | loop fusion | flops 1572864 | bytes 6291462 | tf_op jit(solution)/shard_map/jit(_take)/select_n | solution.py:29
  (7 shorter events, 0.0 us)
Async XLA Ops:
  7.2 1.9 copy-start
  7.2 64.4 %reduce-scatter.2.cloned.1.call-start = ((), (), s32[]{:S(2)}) async-start(), calls=%async_computation.1 | async-start | bytes 3670016 | tf_op jit(solution)/shard_map/reduce_scatter | solution.py:17
  15.5 265.3 %all-gather.3.cloned.1.call-start = ((), (), s32[]{:S(2)}) async-start(), calls=%async_computation.2 | async-start | bytes 3670016 | tf_op jit(solution)/shard_map/all_gather | solution.py:28
  73.7 134.5 %copy-start.3 = (s32[1,6]{1,0:T(1,128)S(1)}, s32[1,6]{1,0:T(1,128)}, u32[]{:S(2)}) copy-start(s32[1,6]{1,0:T(1,128)} %param.9) | copy-start | bytes 76
  208.3 3.2 %copy-start.1 = (bf16[512,512]{1,0:T(8,128)(2,1)S(1)}, bf16[512,512]{1,0:T(8,128)(2,1)}, u32[]{:S(2)}) copy-start(bf16[512,512]{1,0:T(8,128)(2,1)} %all-reduce.1) | copy-start | bytes 1572868
  208.3 3.2 %copy-start.2 = (f32[1,1,512,512]{3,2,1,0:T(8,128)S(1)}, f32[1,1,512,512]{3,2,1,0:T(8,128)}, u32[]{:S(2)}) copy-start(f32[1,1,512,512]{3,2,1,0:T(8,128)} %param.11) | copy-start | bytes 3145732
Sparse Core Ops, SparseCore 0:
  15.7 55.8 reduce-scatter.1
  208.4 72.4 all-gather.2
where the time goes:
time: 296 us
  blocking collectives  128 us (43%)
  waiting for transfers between devices  124 us (42%)
  between operations  14.8 us (5%)
  other arithmetic  13.1 us (4%)
  matrix products  8.39 us (3%)
  local copies, waits for them, and re-layouts  7.83 us (3%)
    psum x1, blocking collectives, local(): owned = lax.psum(mine[0], 'replica').astype(jnp.bfloat16)  128 us
    all_gather x1, waiting for transfers between devices, local(): gathered = lax.all_gather(scaled[None], 'owner', axis=0, tiled=True)  67.9 us
    reduce_scatter x1, waiting for transfers between devices, local(): lax.psum_scatter(ordered.astype(jnp.float32).astype(jnp.bfloat16), 'owner...  56 us
  transfers between devices with their start and end apart: 2, of which 2 were waited for; matrix products, arithmetic and copies ran while one was open for 2% of the time, Pallas kernels for 0%

commit v1 on v0

v1 whole, which is shorter than its diff:
```python
import jax
import jax.numpy as jnp
from jax import lax
from jax.experimental import pallas as pl
from jax.experimental.pallas import tpu as pltpu
from jax.sharding import Mesh, PartitionSpec as P

decay = 0.9
epsilon = 1e-06

NY, NX, NZ, NC, NT = 8, 4, 3, 2, 4
B = 512
ROWS = B // (NX * NY)
SWAP = [(0, 1), (1, 0)]


def assemble_kernel(pick_ref, same_ref, other_ref, out_ref, sem):
    count = out_ref.shape[0]

    def copies(k):
        o = pick_ref[k]
        z = lax.rem(o, NZ)
        return (
            o < NZ,
            pltpu.make_async_copy(same_ref.at[z], out_ref.at[k], sem.at[k]),
            pltpu.make_async_copy(other_ref.at[z], out_ref.at[k], sem.at[k]),
        )

    for k in range(count):
        near, a, b = copies(k)

        @pl.when(near)
        def _():
            a.start()

        @pl.when(jnp.logical_not(near))
        def _():
            b.start()

    for k in range(count):
        _, a, _ = copies(k)
        a.wait()


def assemble(pick, same, other):
    count = pick.shape[0]
    return pl.pallas_call(
        assemble_kernel,
        out_shape=jax.ShapeDtypeStruct((count, B, B), same.dtype),
        in_specs=[
            pl.BlockSpec(memory_space=pltpu.SMEM),
            pl.BlockSpec(memory_space=pltpu.VMEM),
            pl.BlockSpec(memory_space=pltpu.VMEM),
        ],
        out_specs=pl.BlockSpec(memory_space=pl.ANY),
        scratch_shapes=[pltpu.SemaphoreType.DMA((count,))],
        name="assemble",
    )(pick, same, other)


def local(grad_partial, owner_table, left_factor, right_factor, left_precond, right_precond):
    table_row = owner_table[0]
    core = lax.axis_index("core")
    count = table_row.shape[0]
    positions = jnp.arange(count, dtype=jnp.int32)
    slot = positions % NZ
    wanted = 2 * slot + jnp.where(positions < NZ, core, 1 - core)
    matches = table_row[None, :] == wanted[:, None]
    source = jnp.sum(jnp.where(matches, positions[None, :], 0), axis=1)
    pick = table_row // 2 + jnp.where(table_row % 2 == core, 0, NZ)

    grad = grad_partial[0]
    keep = grad.at[source[:NZ]].get(mode="promise_in_bounds")
    give = grad.at[source[NZ:]].get(mode="promise_in_bounds")
    got = lax.ppermute(give, "core", SWAP)
    pair = (keep.astype(jnp.float32) + got.astype(jnp.float32)).astype(jnp.bfloat16)
    pieces = pair.reshape(NZ, NX, NY, ROWS, B).transpose(1, 2, 0, 3, 4)
    over_x = lax.all_to_all(pieces.reshape(NX, NY * NZ * ROWS, B), "x", 0, 0)
    part = jnp.sum(over_x.astype(jnp.float32), axis=0).astype(jnp.bfloat16)
    over_yz = lax.all_to_all(part.reshape(NY * NZ, ROWS, B), ("y", "zl"), 0, 0)
    mine = jnp.sum(over_yz.astype(jnp.float32), axis=0).astype(jnp.bfloat16)

    strip = lax.all_gather(mine, "y", axis=0, tiled=True)
    owned = lax.all_gather(strip, "x", axis=0, tiled=True)

    half_product = jnp.dot(left_precond[0, 0], owned, preferred_element_type=jnp.float32).astype(
        jnp.bfloat16
    )
    full_product = jnp.dot(half_product, right_precond[0, 0], preferred_element_type=jnp.float32)
    scaled = (full_product * lax.rsqrt(jnp.mean(full_product * full_product) + epsilon)).astype(
        jnp.bfloat16
    )
    same = lax.all_to_all(jnp.broadcast_to(scaled[None], (NZ, B, B)), "zl", 0, 0)
    other = lax.ppermute(same, "core", SWAP)
    direction = assemble(pick, same, other)

    outer_rows = lax.dot_general(
        owned, owned, (((1,), (1,)), ((), ())), preferred_element_type=jnp.float32
    )
    outer_cols = lax.dot_general(
        owned, owned, (((0,), (0,)), ((), ())), preferred_element_type=jnp.float32
    )
    new_left = (decay * left_factor[0, 0] + (1.0 - decay) * outer_rows)[None, None]
    new_right = (decay * right_factor[0, 0] + (1.0 - decay) * outer_cols)[None, None]
    return (direction, new_left, new_right)


def solution(mesh):
    fine = Mesh(mesh.devices.reshape(NY, NX, NZ, NC, NT), ("y", "x", "zl", "core", "tensor"))
    owner = ("zl", "core")
    placed = (
        P(("y", "x") + owner, "tensor", None, None),
        P("tensor", None),
        P(owner, "tensor", None, None),
        P(owner, "tensor", None, None),
        P(owner, "tensor", None, None),
        P(owner, "tensor", None, None),
    )
    return jax.shard_map(
        local,
        mesh=fine,
        in_specs=placed,
        out_specs=(
            P("tensor", None, None),
            P(owner, "tensor", None, None),
            P(owner, "tensor", None, None),
        ),
        check_vma=False,
    )
```

time: 296 us -> 140 us (0.47)
  waiting for transfers between devices: 124 us -> 1.5 us
  blocking collectives: 128 us -> 88 us
  starting transfers between devices: 0.08 us -> 25.6 us
  between operations: 14.8 us -> 1.43 us
  other arithmetic: 13.1 us -> 7.84 us
  Pallas kernels: 0 us -> 3.61 us
  local copies, waits for them, and re-layouts: 7.83 us -> 4.76 us
    psum x1 -> x0, blocking collectives: 128 us -> none  [local(): owned = lax.psum(mine[0], 'replica').astype(jnp.bfloat16)]
    all_gather x1 -> x0, waiting for transfers between devices: 67.9 us -> none  [local(): gathered = lax.all_gather(scaled[None], 'owner', axis=0, tiled=True)]
    all_to_all x0 -> x3, blocking collectives: none -> 58.8 us  [the longest x1 23.6 us: local(): over_x = lax.all_to_all(pieces.reshape(NX, NY * NZ * ROWS, B), 'x', 0, 0)]
    reduce_scatter x1 -> x0, waiting for transfers between devices: 56 us -> none  [local(): lax.psum_scatter(ordered.astype(jnp.float32).astype(jnp.bfloat16), 'owner...]
    all_gather x0 -> x2, blocking collectives: none -> 29.2 us  [the longest x1 18.3 us: local(): strip = lax.all_gather(mine, 'y', axis=0, tiled=True)]
    ppermute x0 -> x2, starting transfers between devices: none -> 25.6 us  [the longest x1 13.3 us: local(): other = lax.ppermute(same, 'core', SWAP)]
    select_n x4 -> x1, other arithmetic: 7.85 us -> 0.08 us  [local(): keep = grad.at[source[:NZ]].get(mode='promise_in_bounds')]
    pallas_call x0 -> x1, Pallas kernels: none -> 3.61 us  [assemble(): pl.pallas_call(assemble_kernel, out_shape=jax.ShapeDtypeStruct((count, B,...]
  transfers between devices with their start and end apart: 2 -> 2, of which waited for: 2 -> 1; matrix products, arithmetic and copies ran while one was open for 2% -> 4% of each run, Pallas kernels for 0% -> 0%
where the time goes in v1:
time: 140 us
  blocking collectives  88 us (63%)
  starting transfers between devices  25.6 us (18%)
  other arithmetic  7.84 us (6%)
  matrix products  6.74 us (5%)
  local copies, waits for them, and re-layouts  4.76 us (3%)
  Pallas kernels  3.61 us (3%)
  waiting for transfers between devices  1.5 us (1%)
  between operations  1.43 us (1%)
    all_to_all x1, blocking collectives, local(): over_x = lax.all_to_all(pieces.reshape(NX, NY * NZ * ROWS, B), 'x', 0, 0)  23.6 us
    all_to_all x1, blocking collectives, local(): lax.all_to_all(jnp.broadcast_to(scaled[None], (NZ, B, B)), 'zl', 0, 0)  19 us
    all_gather x1, blocking collectives, local(): strip = lax.all_gather(mine, 'y', axis=0, tiled=True)  18.3 us
    all_to_all x1, blocking collectives, local(): over_yz = lax.all_to_all(part.reshape(NY * NZ, ROWS, B), ('y', 'zl'), 0, 0)  16.2 us
    ppermute x1, starting transfers between devices, local(): other = lax.ppermute(same, 'core', SWAP)  13.3 us
    ppermute x1, starting transfers between devices, local(): got = lax.ppermute(give, 'core', SWAP)  12.4 us
    all_gather x1, blocking collectives, local(): owned = lax.all_gather(strip, 'x', axis=0, tiled=True)  10.9 us
    dot_general x1, matrix products, local(): jnp.dot(half_product, right_precond[0, 0], preferred_element_type=jnp.flo...  3.84 us
  transfers between devices with their start and end apart: 2, of which 1 were waited for; matrix products, arithmetic and copies ran while one was open for 4% of the time, Pallas kernels for 0%

profile of v1, /device:TPU:1, one launch (start us, length us, event | category | flops | bytes accessed | tf_op | source)
XLA Modules:
  0.0 139.5 jit_solution(7826133925638408430)
XLA Ops:
  0.7 1.0 select_reduce_fusion
  1.7 0.1 compare_select_fusion.1
  1.7 0.8 copy-done
  2.5 1.8 %gather_fusion.1 = bf16[3,512,512]{2,1,0:T(8,128)(2,1)} fusion(bf16[6,512,512]{2,1,0:T(8,128)(2,1)S(1)} %bitcast.33, s32[1024]{0:T(1024)S(1)} %pad_clamp_fusion), kind=kCustom, calls=%fused_computation.1 | custom fusion | bytes 3145740 | tf_op jit(solution)/shard_map/gather | solution.py:74
  4.4 12.4 %collective-permute-start = (bf16[3,512,512]{2,1,0:T(8,128)(2,1)}, bf16[3,512,512]{2,1,0:T(8,128)(2,1)}, u32[]{:S(2)}, u32[]{:S(2)}) collective-permute-start(bf16[3,512,512]{2,1,0:T(8,128)(2,1)} %gather_fusion.1), channel_id=1, source_target_pairs={{0,4},{4,0},{1,5},{5,1},{2,6},{6,2},{3,7},{7,3},{8,12},{12,8},{9,1... | collective-permute-start | bytes 4718600 | tf_op jit(solution)/shard_map/ppermute | solution.py:75
  16.8 1.8 %gather_fusion = bf16[3,512,512]{2,1,0:T(8,128)(2,1)} fusion(bf16[6,512,512]{2,1,0:T(8,128)(2,1)S(1)} %bitcast.32, s32[1024]{0:T(1024)S(1)} %pad_clamp_fusion.1), kind=kCustom, calls=%fused_computation | custom fusion | bytes 3145740 | tf_op jit(solution)/shard_map/gather | solution.py:73
  18.6 1.5 %collective-permute-done = bf16[3,512,512]{2,1,0:T(8,128)(2,1)} collective-permute-done((bf16[3,512,512]{2,1,0:T(8,128)(2,1)}, bf16[3,512,512]{2,1,0:T(8,128)(2,1)}, u32[]{:S(2)}, u32[]{:S(2)}) %collective-permute-start) | collective-permute-done | bytes 1572896 | tf_op jit(solution)/shard_map/ppermute | solution.py:75
  20.1 2.3 %add_convert_fusion = bf16[3,512,512]{2,1,0:T(8,128)(2,1)S(1)} fusion(bf16[3,512,512]{2,1,0:T(8,128)(2,1)} %collective-permute-done, bf16[3,512,512]{2,1,0:T(8,128)(2,1)} %gather_fusion), kind=kLoop, calls=%fused_computation.2 | loop fusion | flops 3145728 | bytes 4718592 | tf_op jit(solution)/shard_map/convert_element_type | solution.py:76
  22.4 0.1 copy.10
  22.6 23.6 %all_to_all.15 = bf16[4,384,512]{2,1,0:T(8,128)(2,1)} all-to-all(bf16[4,384,512]{2,1,0:T(8,128)(2,1)S(1)} %bitcast.34), channel_id=1, replica_groups=mesh['y'=8,'x'=4,'zl'=3,'core'=2,'tensor'=4] {'x'}, dimensions={0} | all-to-all | bytes 3145728 | tf_op jit(solution)/shard_map/all_to_all | solution.py:78
  46.2 2.5 %reduce_sum.43 = bf16[384,512]{1,0:T(8,128)(2,1)} reduce(bf16[4,384,512]{2,1,0:T(8,128)(2,1)} %all_to_all.15, bf16[]{:T(256)} %constant.55.clone.1), dimensions={0}, to_apply=%region_1.2 | reduce | flops 589824 | bytes 1966082 | tf_op jit(solution)/shard_map/reduce_sum | solution.py:79
  48.7 16.2 %all_to_all.16 = bf16[24,16,512]{2,1,0:T(8,128)(2,1)S(1)} all-to-all(bf16[24,16,512]{2,1,0:T(8,128)(2,1)} %bitcast.36), channel_id=1, replica_groups=mesh['y'=8,'x'=4,'zl'=3,'core'=2,'tensor'=4] {'y','zl'}, dimensions={0} | all-to-all | bytes 786432 | tf_op jit(solution)/shard_map/all_to_all | solution.py:80
  64.9 0.1 reduce_sum.44
  65.0 18.3 %all_gather.6 = bf16[128,512]{1,0:T(8,128)(2,1)S(1)} all-gather(bf16[16,512]{1,0:T(8,128)(2,1)S(1)} %reduce_sum.44), channel_id=1, replica_groups=mesh['y'=8,'x'=4,'zl'=3,'core'=2,'tensor'=4] {'y'}, dimensions={0}, use_global_device_ids=true | all-gather | bytes 147456 | tf_op jit(solution)/shard_map/all_gather | solution.py:83
  83.3 10.9 %all_gather.7 = bf16[512,512]{1,0:T(8,128)(2,1)} all-gather(bf16[128,512]{1,0:T(8,128)(2,1)S(1)} %all_gather.6), channel_id=1, replica_groups=mesh['y'=8,'x'=4,'zl'=3,'core'=2,'tensor'=4] {'x'}, dimensions={0}, use_global_device_ids=true | all-gather | bytes 655360 | tf_op jit(solution)/shard_map/all_gather | solution.py:84
  94.2 3.8 %multiply_reduce_fusion = (f32[]{:T(128)}, f32[512,512]{1,0:T(8,128)}) fusion(bf16[1,1,512,512]{3,2,1,0:T(8,128)(2,1)} %param.11, bf16[512,512]{1,0:T(8,128)(2,1)} %all_gather.7, bf16[1,1,512,512]{3,2,1,0:T(8,128)(2,1)} %param.10), kind=kOutput, calls=%fused_computation.12 | convolution fusion | flops 537657344 | bytes 2621444 | tf_op jit(solution)/shard_map/dot_general | solution.py:89
  98.7 1.3 multiply_convert_fusion
  100.0 0.1 broadcast_in_dim.50
  100.2 19.0 %all_to_all.17.same_ref = bf16[3,512,512]{2,1,0:T(8,128)(2,1)S(1)} all-to-all(bf16[3,512,512]{2,1,0:T(8,128)(2,1)S(1)} %broadcast_in_dim.50), channel_id=1, replica_groups=mesh['y'=8,'x'=4,'zl'=3,'core'=2,'tensor'=4] {'zl'}, dimensions={0} | all-to-all | bytes 3145728 | tf_op jit(solution)/shard_map/all_to_all | solution.py:93
  119.2 13.3 %collective-permute-start.1 = (bf16[3,512,512]{2,1,0:T(8,128)(2,1)S(1)}, bf16[3,512,512]{2,1,0:T(8,128)(2,1)}, u32[]{:S(2)}, u32[]{:S(2)}) collective-permute-start(bf16[3,512,512]{2,1,0:T(8,128)(2,1)S(1)} %all_to_all.17.same_ref), channel_id=1, source_target_pairs={{0,4},{4,0},{1,5},{5,1},{2,6},{6,2},{3,7},{7,3},{8,12},{12,8},{9,1... | collective-permute-start | bytes 4718600 | tf_op jit(solution)/shard_map/ppermute | solution.py:94
  132.5 0.5 fusion.8.pick_ref
  133.0 1.4 %fusion.3 = f32[1,1,512,512]{3,2,1,0:T(8,128)} fusion(bf16[512,512]{1,0:T(8,128)(2,1)S(1)} %copy-done.1, f32[1,1,512,512]{3,2,1,0:T(8,128)S(1)} %copy-done.3), kind=kOutput, calls=%fused_computation.8 | convolution fusion | flops 269221888 | bytes 2621440 | tf_op jit(solution)/shard_map/dot_general | solution.py:97
  134.4 1.5 %fusion.1 = f32[1,1,512,512]{3,2,1,0:T(8,128)} fusion(bf16[512,512]{1,0:T(8,128)(2,1)S(1)} %copy-done.1, f32[1,1,512,512]{3,2,1,0:T(8,128)S(1)} %copy-done.4), kind=kOutput, calls=%fused_computation.5 | convolution fusion | flops 269221888 | bytes 2621440 | tf_op jit(solution)/shard_map/dot_general | solution.py:100
  135.9 3.6 %assemble.1 = bf16[6,512,512]{2,1,0:T(8,128)(2,1)} custom-call(s32[6]{0:T(128)} %fusion.8.pick_ref, bf16[3,512,512]{2,1,0:T(8,128)(2,1)} %copy-done.2, bf16[3,512,512]{2,1,0:T(8,128)(2,1)} %collective-permute-done.1.other_ref), custom_call_target="tpu_custom_call" | custom-call | tf_op jit(solution)/shard_map/assemble/pallas_call | solution.py:47
  (15 shorter events, 0.1 us)
Async XLA Ops:
  0.6 1.9 %copy-start = (bf16[1,6,512,512]{3,2,1,0:T(8,128)(2,1)S(1)}, bf16[1,6,512,512]{3,2,1,0:T(8,128)(2,1)}, u32[]{:S(2)}) copy-start(bf16[1,6,512,512]{3,2,1,0:T(8,128)(2,1)} %param.6) | copy-start | bytes 9437188
  4.4 15.7 %collective-permute-start = (bf16[3,512,512]{2,1,0:T(8,128)(2,1)}, bf16[3,512,512]{2,1,0:T(8,128)(2,1)}, u32[]{:S(2)}, u32[]{:S(2)}) collective-permute-start(bf16[3,512,512]{2,1,0:T(8,128)(2,1)} %gather_fusion.1), channel_id=1, source_target_pairs={{0,4},{4,0},{1,5},{5,1},{2,6},{6,2},{3,7},{7,3},{8,12},{12,8},{9,1... | collective-permute-start | bytes 4718600 | tf_op jit(solution)/shard_map/ppermute | solution.py:75
  100.2 32.3 %copy-start.5 = (s32[1,6]{1,0:T(1,128)S(1)}, s32[1,6]{1,0:T(1,128)}, u32[]{:S(2)}) copy-start(s32[1,6]{1,0:T(1,128)} %param.7) | copy-start | bytes 76
  100.2 32.8 %copy-start.1 = (bf16[512,512]{1,0:T(8,128)(2,1)S(1)}, bf16[512,512]{1,0:T(8,128)(2,1)}, u32[]{:S(2)}) copy-start(bf16[512,512]{1,0:T(8,128)(2,1)} %all_gather.7) | copy-start | bytes 1572868
  100.2 32.8 %copy-start.3 = (f32[1,1,512,512]{3,2,1,0:T(8,128)S(1)}, f32[1,1,512,512]{3,2,1,0:T(8,128)}, u32[]{:S(2)}) copy-start(f32[1,1,512,512]{3,2,1,0:T(8,128)} %param.8) | copy-start | bytes 3145732
  119.2 15.3 %copy-start.2 = (bf16[3,512,512]{2,1,0:T(8,128)(2,1)}, bf16[3,512,512]{2,1,0:T(8,128)(2,1)S(1)}, u32[]{:S(2)}) copy-start(bf16[3,512,512]{2,1,0:T(8,128)(2,1)S(1)} %all_to_all.17.same_ref) | copy-start | bytes 4718596
  119.2 16.7 %collective-permute-start.1 = (bf16[3,512,512]{2,1,0:T(8,128)(2,1)S(1)}, bf16[3,512,512]{2,1,0:T(8,128)(2,1)}, u32[]{:S(2)}, u32[]{:S(2)}) collective-permute-start(bf16[3,512,512]{2,1,0:T(8,128)(2,1)S(1)} %all_to_all.17.same_ref), channel_id=1, source_target_pairs={{0,4},{4,0},{1,5},{5,1},{2,6},{6,2},{3,7},{7,3},{8,12},{12,8},{9,1... | collective-permute-start | bytes 4718600 | tf_op jit(solution)/shard_map/ppermute | solution.py:94
  133.0 1.5 %copy-start.4 = (f32[1,1,512,512]{3,2,1,0:T(8,128)S(1)}, f32[1,1,512,512]{3,2,1,0:T(8,128)}, u32[]{:S(2)}) copy-start(f32[1,1,512,512]{3,2,1,0:T(8,128)} %param.9) | copy-start | bytes 3145732
